TPU v7x, 32 devices: a whole 2x2x4 slice. The times are simulated.
32 devices in a mesh: dp: 8 (over y, x, core), tensor: 4 (over z).
Axes of the slice: x: 2, y: 2, z: 4, core: 2. Of those that a mesh axis runs over, the one named last changes fastest.
Arguments:
- tokens: bfloat16 [20480, 768], P(('dp', 'tensor')), may hold values from -6 to 6
- visible_counts: int32 [256], P('dp'), may hold values from 20 to 78, as said below
- norm_one_gain: float32 [768], replicated, may hold values from 0.1 to 1.9
- norm_one_shift: float32 [768], replicated, may hold values from -1.8 to 1.8
- input_weight: bfloat16 [768, 3, 768], P(None, None, 'tensor'), may hold values from -0.21875 to 0.21875
- input_bias: bfloat16 [2, 768], P(None, 'tensor'), may hold values from -1.796875 to 1.796875
- mixer_weight: bfloat16 [768, 768], P('tensor'), may hold values from -1.25 to 1.25
- mixer_bias: float32 [768], replicated, may hold values from -1.8 to 1.8
- norm_two_gain: float32 [768], replicated, may hold values from 0.1 to 1.9
- norm_two_shift: float32 [768], replicated, may hold values from -1.8 to 1.8
- up_weight: bfloat16 [768, 3072], P(None, 'tensor'), may hold values from -0.21875 to 0.21875
- up_bias: bfloat16 [3072], P('tensor'), may hold values from -1.796875 to 1.796875
- down_weight: bfloat16 [3072, 768], P('tensor'), may hold values from -0.109375 to 0.109375
- down_bias: float32 [768], replicated, may hold values from -1.8 to 1.8
- output_grad: bfloat16 [20480, 768], P(('dp', 'tensor')), may hold values from -6 to 6
Outputs:
- block_output: bfloat16 [20480, 768], P(('dp', 'tensor'))
- grad_tokens: float32 [20480, 768], P(('dp', 'tensor'))
- grad_norm_one_gain: float32 [768], replicated
- grad_norm_one_shift: float32 [768], replicated
- grad_input_weight: float32 [768, 3, 768], P(None, None, 'tensor')
- grad_input_bias: float32 [2, 768], P(None, 'tensor')
- grad_mixer_weight: float32 [768, 768], P('tensor')
- grad_mixer_bias: float32 [768], replicated
- grad_norm_two_gain: float32 [768], replicated
- grad_norm_two_shift: float32 [768], replicated
- grad_up_weight: float32 [768, 3072], P(None, 'tensor')
- grad_up_bias: float32 [3072], P('tensor')
- grad_down_weight: float32 [3072, 768], P('tensor')
- grad_down_bias: float32 [768], replicated
Inputs may be any that keep to these rules, and one draw needn't show every extreme that they name: `visible_counts`: each image has 20 to 78 visible patches; some image has exactly 78 and some exactly 20.
All inputs are finite; a program needn't handle non-finite values.
Results may differ from a plain program's by a relative error of at most 0.014.
Values may be sent and summed in bfloat16 or wider, within the bound.
No kernel may reach another device: no remote copies, remote signals or barrier semaphores. Data moves between devices by JAX's collectives and lax.ppermute only.
A program may use at most 128 MiB of HBM per device.

v0:
```python
import jax
import jax.numpy as jnp
from jax import lax
from jax.sharding import PartitionSpec as P

HD = 64
SLOTS = 80
masked_score = -1000000000.0


def layer_norm(inputs, norm_gain, norm_shift):
    center = inputs - jnp.mean(inputs, axis=-1, keepdims=True)
    spread = jnp.mean(center * center, axis=-1, keepdims=True)
    return center * lax.rsqrt(spread + 1e-06) * norm_gain + norm_shift


def norm_back(inputs, norm_gain, norm_shift, grad_normed):
    unused, pullback = jax.vjp(layer_norm, inputs, norm_gain, norm_shift)
    return pullback(grad_normed)


def gelu_exact(inputs):
    return jax.nn.gelu(inputs, approximate=False)


def split_heads(flat, slot_count, head_dim):
    return flat.reshape(
        flat.shape[0] // slot_count, slot_count, flat.shape[1] // head_dim, head_dim
    )


def visible_keys(counts, slot_count):
    return (lax.broadcasted_iota(jnp.int32, (counts.shape[0], slot_count), 1) < counts[:, None])[
        :, None, None, :
    ]


def project_inputs(normed_rows, weight_in, bias_in, slot_count, head_dim):
    columns = weight_in.shape[2]
    product = jnp.dot(
        normed_rows,
        weight_in.reshape(weight_in.shape[0], 3 * columns),
        preferred_element_type=jnp.float32,
    ).reshape(-1, 3, columns)
    queries = (product[:, 0] + bias_in[0]).astype(jnp.bfloat16)
    key_rows = product[:, 1].astype(jnp.bfloat16)
    values = (product[:, 2] + bias_in[1]).astype(jnp.bfloat16)
    return (
        split_heads(queries, slot_count, head_dim),
        split_heads(key_rows, slot_count, head_dim),
        split_heads(values, slot_count, head_dim),
    )


def attend(queries, key_rows, values, counts):
    factor = queries.shape[-1] ** (-0.5)
    scores = (
        jnp.einsum("bqhd,bkhd->bhqk", queries, key_rows, preferred_element_type=jnp.float32)
        * factor
    )
    scores = jnp.where(visible_keys(counts, key_rows.shape[1]), scores, masked_score)
    maxima = jnp.max(scores, axis=-1, keepdims=True)
    exponent = jnp.exp(scores - maxima)
    totals = jnp.sum(exponent, axis=-1, keepdims=True)
    soft_low = (exponent / totals).astype(jnp.bfloat16)
    blended = jnp.einsum("bhqk,bkhd->bqhd", soft_low, values, preferred_element_type=jnp.float32)
    return (blended, maxima + jnp.log(totals))


def attend_back(queries, key_rows, values, counts, log_totals, grad_blend):
    factor = queries.shape[-1] ** (-0.5)
    scores = (
        jnp.einsum("bqhd,bkhd->bhqk", queries, key_rows, preferred_element_type=jnp.float32)
        * factor
    )
    scores = jnp.where(visible_keys(counts, key_rows.shape[1]), scores, masked_score)
    soft = jnp.exp(scores - log_totals)
    soft_low = soft.astype(jnp.bfloat16)
    grad_values = jnp.einsum(
        "bhqk,bqhd->bkhd", soft_low, grad_blend, preferred_element_type=jnp.float32
    )
    grad_soft = jnp.einsum(
        "bqhd,bkhd->bhqk", grad_blend, values, preferred_element_type=jnp.float32
    )
    grad_scores = soft * (grad_soft - jnp.sum(grad_soft * soft, axis=-1, keepdims=True))
    grad_low = grad_scores.astype(jnp.bfloat16)
    grad_queries = (
        jnp.einsum("bhqk,bkhd->bqhd", grad_low, key_rows, preferred_element_type=jnp.float32)
        * factor
    )
    grad_keys = (
        jnp.einsum("bhqk,bqhd->bkhd", grad_low, queries, preferred_element_type=jnp.float32)
        * factor
    )
    return (grad_queries, grad_keys, grad_values)


def mlp_back(normed_rows, hidden_pre, active, grad_rows, weight_down):
    grad_down = jnp.einsum("rf,rd->fd", active, grad_rows, preferred_element_type=jnp.float32)
    grad_active = jnp.einsum(
        "rd,fd->rf", grad_rows, weight_down, preferred_element_type=jnp.float32
    )
    unused, pullback = jax.vjp(gelu_exact, hidden_pre)
    grad_pre = pullback(grad_active)[0]
    grad_up_b = jnp.sum(grad_pre, axis=0)
    grad_pre_low = grad_pre.astype(jnp.bfloat16)
    grad_up = jnp.einsum("rd,rf->df", normed_rows, grad_pre_low, preferred_element_type=jnp.float32)
    return (grad_down, grad_up, grad_up_b, grad_pre_low)


def mixer_back(
    normed_rows,
    queries,
    key_rows,
    values,
    counts,
    log_totals,
    grad_rows,
    blend_low,
    weight_mix,
    slot_count,
    head_dim,
):
    row_total = blend_low.shape[0]
    grad_mix = jnp.einsum("rc,rd->cd", blend_low, grad_rows, preferred_element_type=jnp.float32)
    grad_blend = jnp.einsum(
        "rd,cd->rc", grad_rows, weight_mix, preferred_element_type=jnp.float32
    ).astype(jnp.bfloat16)
    grad_queries, grad_keys, grad_values = attend_back(
        queries, key_rows, values, counts, log_totals, split_heads(grad_blend, slot_count, head_dim)
    )
    grad_queries = grad_queries.reshape(row_total, -1)
    grad_keys = grad_keys.reshape(row_total, -1)
    grad_values = grad_values.reshape(row_total, -1)
    grad_bias_in = jnp.stack([jnp.sum(grad_queries, axis=0), jnp.sum(grad_values, axis=0)])
    grad_projected = jnp.stack([grad_queries, grad_keys, grad_values], axis=1).astype(jnp.bfloat16)
    grad_weight_in = jnp.einsum(
        "rd,rjc->djc", normed_rows, grad_projected, preferred_element_type=jnp.float32
    )
    return (grad_mix, grad_bias_in, grad_weight_in, grad_projected)


def local(
    tokens,
    visible_counts,
    norm_one_gain,
    norm_one_shift,
    input_weight,
    input_bias,
    mixer_weight,
    mixer_bias,
    norm_two_gain,
    norm_two_shift,
    up_weight,
    up_bias,
    down_weight,
    down_bias,
    output_grad,
):
    slot_count = SLOTS
    head_dim = HD
    inputs = tokens.astype(jnp.float32)
    grad_output = output_grad.astype(jnp.float32)
    low_one = layer_norm(inputs, norm_one_gain, norm_one_shift).astype(jnp.bfloat16)
    whole_one = lax.all_gather(low_one, "tensor", axis=0, tiled=True)
    queries, key_rows, values = project_inputs(
        whole_one, input_weight, input_bias, slot_count, head_dim
    )
    blended, log_totals = attend(queries, key_rows, values, visible_counts)
    blend_low = blended.reshape(whole_one.shape[0], -1).astype(jnp.bfloat16)
    first_sum = (
        inputs
        + lax.psum_scatter(
            jnp.dot(blend_low, mixer_weight, preferred_element_type=jnp.float32),
            "tensor",
            scatter_dimension=0,
            tiled=True,
        )
        + mixer_bias
    )
    low_two = layer_norm(first_sum, norm_two_gain, norm_two_shift).astype(jnp.bfloat16)
    whole_two = lax.all_gather(low_two, "tensor", axis=0, tiled=True)
    hidden_pre = jnp.dot(whole_two, up_weight, preferred_element_type=jnp.float32) + up_bias
    active = gelu_exact(hidden_pre).astype(jnp.bfloat16)
    result = (
        first_sum
        + lax.psum_scatter(
            jnp.dot(active, down_weight, preferred_element_type=jnp.float32).astype(jnp.bfloat16),
            "tensor",
            scatter_dimension=0,
            tiled=True,
        ).astype(jnp.float32)
        + down_bias
    )
    whole_grad = lax.all_gather(output_grad, "tensor", axis=0, tiled=True)
    grad_down, grad_up, grad_up_b, grad_pre_low = mlp_back(
        whole_two, hidden_pre, active, whole_grad, down_weight
    )
    grad_normed_two = lax.psum_scatter(
        jnp.einsum("rf,df->rd", grad_pre_low, up_weight, preferred_element_type=jnp.float32),
        "tensor",
        scatter_dimension=0,
        tiled=True,
    )
    grad_first, grad_gain_two, grad_shift_two = norm_back(
        first_sum, norm_two_gain, norm_two_shift, grad_normed_two
    )
    grad_first = grad_output + grad_first
    whole_first = lax.all_gather(grad_first.astype(jnp.bfloat16), "tensor", axis=0, tiled=True)
    grad_mix, grad_bias_in, grad_weight_in, grad_projected = mixer_back(
        whole_one,
        queries,
        key_rows,
        values,
        visible_counts,
        log_totals,
        whole_first,
        blend_low,
        mixer_weight,
        slot_count,
        head_dim,
    )
    grad_normed_one = lax.psum_scatter(
        jnp.einsum(
            "rjc,djc->rd", grad_projected, input_weight, preferred_element_type=jnp.float32
        ).astype(jnp.bfloat16),
        "tensor",
        scatter_dimension=0,
        tiled=True,
    ).astype(jnp.float32)
    weight_terms = (grad_weight_in, grad_bias_in, grad_mix, grad_up, grad_up_b, grad_down)
    grad_inputs, grad_gain_one, grad_shift_one = norm_back(
        inputs, norm_one_gain, norm_one_shift, grad_normed_one
    )
    grad_tokens = grad_first + grad_inputs
    sum_gain_one, sum_shift_one, sum_mix_bias, sum_gain_two, sum_shift_two, sum_down_bias = (
        lax.psum(
            (
                grad_gain_one,
                grad_shift_one,
                jnp.sum(grad_first, axis=0),
                grad_gain_two,
                grad_shift_two,
                jnp.sum(grad_output, axis=0),
            ),
            ("dp", "tensor"),
        )
    )
    sum_weight_in, sum_bias_in, sum_mix, sum_up, sum_up_b, sum_down = lax.psum(
        (
            weight_terms[0],
            weight_terms[1],
            weight_terms[2],
            weight_terms[3],
            weight_terms[4],
            weight_terms[5],
        ),
        "dp",
    )
    return (
        result.astype(jnp.bfloat16),
        grad_tokens,
        sum_gain_one,
        sum_shift_one,
        sum_weight_in,
        sum_bias_in,
        sum_mix,
        sum_mix_bias,
        sum_gain_two,
        sum_shift_two,
        sum_up,
        sum_up_b,
        sum_down,
        sum_down_bias,
    )


def solution(mesh):
    in_specs = (
        P(("dp", "tensor"), None),
        P("dp"),
        P(),
        P(),
        P(None, None, "tensor"),
        P(None, "tensor"),
        P("tensor", None),
        P(),
        P(),
        P(),
        P(None, "tensor"),
        P("tensor"),
        P("tensor", None),
        P(),
        P(("dp", "tensor"), None),
    )
    out_specs = (
        P(("dp", "tensor"), None),
        P(("dp", "tensor"), None),
        P(),
        P(),
        P(None, None, "tensor"),
        P(None, "tensor"),
        P("tensor", None),
        P(),
        P(),
        P(),
        P(None, "tensor"),
        P("tensor"),
        P("tensor", None),
        P(),
    )
    return jax.shard_map(local, mesh=mesh, in_specs=in_specs, out_specs=out_specs, check_vma=False)
```

profile of v0, /device:TPU:0, one launch (start us, length us, event | category | flops | bytes accessed | tf_op | source)
XLA Modules:
  0.0 1010.1 jit_solution(16693348201039939642)
XLA Ops:
  14.6 79.0 %all-gather.5.cloned.1.call-done = bf16[2560,768]{1,0:T(8,128)(2,1)} async-done(((bf16[640,768]{1,0:T(8,128)(2,1)}), bf16[2560,768]{1,0:T(8,128)(2,1)}) %all-gather.5.cloned.1.call-update) | async-done | bytes 3932176 | tf_op jit(solution)/shard_map/all_gather | solution.py:165
  93.6 4.6 fusion.6
  104.7 4.7 squeeze.4
  109.4 4.1 squeeze.10
  113.5 5.2 fusion.57
  130.9 4.3 fusion.58
  135.3 134.9 %reduce-scatter.5.cloned.1.call-done = f32[640,768]{1,0:T(8,128)} async-done(((f32[2560,768]{1,0:T(8,128)}), f32[640,768]{1,0:T(8,128)}) %reduce-scatter.5.cloned.1.call-update) | async-done | bytes 1966096 | tf_op jit(solution)/shard_map/reduce_scatter | solution.py:173
  274.7 76.5 %all-gather.7.cloned.1.call-done = bf16[2560,768]{1,0:T(8,128)(2,1)} async-done(((bf16[640,768]{1,0:T(8,128)(2,1)}), bf16[2560,768]{1,0:T(8,128)(2,1)}) %all-gather.7.cloned.1.call-update) | async-done | bytes 3932176 | tf_op jit(solution)/shard_map/all_gather | solution.py:182
  351.2 9.0 fusion.59
  360.2 67.5 %all-gather.9.cloned.1.call-done = bf16[2560,768]{1,0:T(8,128)(2,1)} async-done(((bf16[640,768]{1,0:T(8,128)(2,1)}), bf16[2560,768]{1,0:T(8,128)(2,1)}) %all-gather.9.cloned.1.call-update) | async-done | bytes 3932176 | tf_op jit(solution)/shard_map/all_gather | solution.py:195
  427.6 23.8 %fusion.51 = (f32[768]{0:T(1024)S(1)}, bf16[2560,768]{1,0:T(8,128)(2,1)S(1)}, f32[2560,768]{1,0:T(8,128)}) fusion(f32[2560,768]{1,0:T(8,128)} %fusion.59, f32[768]{0:T(1024)S(1)} %convert_element_type.88, bf16[2560,768]{1,0:T(8,128)(2,1)} %all-gather.9.cloned.1.call-done, bf16[768,768]{1,0:T(8,128)(2,1)S(1)} %copy-done), kind=kOutput, calls=%fused_computation.106 | convolution fusion | flops 3165388032 | bytes 24778752 | tf_op jit(solution)/shard_map/rd,fd->rf/dot_general | solution.py:100
  453.3 5.4 fusion.29
  459.2 8.0 multiply_convert_fusion
  469.2 4.7 convolution_convert_fusion
  473.9 119.7 %reduce-scatter.9.cloned.1.call-done = f32[640,768]{1,0:T(8,128)} async-done(((f32[2560,768]{1,0:T(8,128)}), f32[640,768]{1,0:T(8,128)}) %reduce-scatter.9.cloned.1.call-update) | async-done | bytes 1966096 | tf_op jit(solution)/shard_map/reduce_scatter | solution.py:199
  596.0 73.1 %reduce-scatter.7.cloned.1.call-done = bf16[640,768]{1,0:T(8,128)(2,1)} async-done(((bf16[2560,768]{1,0:T(8,128)(2,1)}), bf16[640,768]{1,0:T(8,128)(2,1)}) %reduce-scatter.7.cloned.1.call-update) | async-done | bytes 983056 | tf_op jit(solution)/shard_map/reduce_scatter | solution.py:187
  669.0 3.7 fusion.53
  675.4 76.9 %all-gather.11.cloned.1.call-done = bf16[2560,768]{1,0:T(8,128)(2,1)} async-done(((bf16[640,768]{1,0:T(8,128)(2,1)}), bf16[2560,768]{1,0:T(8,128)(2,1)}) %all-gather.11.cloned.1.call-update) | async-done | bytes 3932176 | tf_op jit(solution)/shard_map/all_gather | solution.py:209
  752.2 4.5 convolution_convert_fusion.1
  760.0 7.1 multiply_reduce_fusion
  772.0 4.0 fusion.33
  780.6 3.9 stack_reshape.14
  786.9 3.7 stack_reshape.13
  793.0 3.7 stack_reshape.12
  800.9 4.7 bitcast_convert_fusion
  806.0 8.1 fusion.27
  814.2 4.8 fusion.61
  820.9 3.7 fusion.62
  829.5 14.4 %all-reduce.1 = (f32[2,192]{1,0:T(2,128)}, f32[768]{0:T(1024)}) all-reduce(f32[2,192]{1,0:T(2,128)S(1)} %pad_maximum_fusion, f32[768]{0:T(1024)S(1)} %get-tuple-element.37), channel_id=1, replica_groups=mesh['dp'=8,'tensor'=4] {'dp'}, use_global_device_ids=true, to_apply=%region_22.23 | all-reduce | flops 1152 | bytes 9216 | tf_op jit(solution)/shard_map/psum | solution.py:249
  843.9 33.2 %reduce-scatter.11.cloned.1.call-done = bf16[640,768]{1,0:T(8,128)(2,1)} async-done(((bf16[2560,768]{1,0:T(8,128)(2,1)}), bf16[640,768]{1,0:T(8,128)(2,1)}) %reduce-scatter.11.cloned.1.call-update) | async-done | bytes 983056 | tf_op jit(solution)/shard_map/reduce_scatter | solution.py:223
  883.8 41.7 %all-reduce = (f32[768]{0:T(1024)}, f32[768]{0:T(1024)}, f32[768]{0:T(1024)}, f32[768]{0:T(1024)}, f32[768]{0:T(1024)}, /*index=5*/f32[768]{0:T(1024)}) all-reduce(f32[768]{0:T(1024)S(1)} %get-tuple-element.16, f32[768]{0:T(1024)S(1)} %get-tuple-element.21, ...), channel_id=1, replica_groups=mesh['dp'=8,'tensor'=4] {'dp','tensor'}, use_global_device_ids=true, to_apply=%region_16.17 | all-reduce | flops 4608 | bytes 36864 | tf_op jit(solution)/shard_map/psum | solution.py:237
  925.4 71.1 %all-reduce.5.cloned.1.call-done = (f32[768,3,192]{0,2,1:T(8,128)}, f32[192,768]{1,0:T(8,128)}, f32[768,768]{1,0:T(8,128)}, f32[768,768]{1,0:T(8,128)}) async-done(((f32[768,3,192]{0,2,1:T(8,128)}, f32[192,768]{1,0:T(8,128)}, f32[768,768]{1,0:T(8,128)}, f32[768,768]{1,0:T(8,128)}), (f32[768,3,192]{0,2,1:T(8,128)}, f32[192,768]{1,0:T(8,128)}, f32[768,768]{1,0:T(8,128)}, ...) | async-done | bytes 7077904 | tf_op jit(solution)/shard_map/psum | solution.py:249
  (164 shorter events, 81.8 us)
Async XLA Ops:
  7.2 420.5 %copy-start = (bf16[768,768]{1,0:T(8,128)(2,1)S(1)}, bf16[768,768]{1,0:T(8,128)(2,1)}, u32[]{:S(2)}) copy-start(bf16[768,768]{1,0:T(8,128)(2,1)} %param.27) | copy-start | bytes 3538948
  7.2 7.1 copy-start.38
  7.2 7.3 copy-start.40
  7.2 86.3 %copy-start.44 = (bf16[768,3,192]{0,2,1:T(8,128)(2,1)S(1)}, bf16[768,3,192]{0,2,1:T(8,128)(2,1)}, u32[]{:S(2)}) copy-start(bf16[768,3,192]{0,2,1:T(8,128)(2,1)} %param.19) | copy-start | bytes 2654212
  7.2 86.3 %all-gather.5.cloned.1.call-start = ((), (), s32[]{:S(2)}) async-start(), calls=%async_computation.4 | async-start | bytes 4915200 | tf_op jit(solution)/shard_map/all_gather | solution.py:165
  14.3 255.9 %reduce-scatter.5.cloned.1.call-start = ((), (), s32[]{:S(2)}) async-start(), calls=%async_computation.5 | async-start | bytes 9830400 | tf_op jit(solution)/shard_map/reduce_scatter | solution.py:173
  104.7 8.9 copy-start.7
  118.7 6.3 copy-start.1
  125.1 5.8 copy-start.24
  135.2 135.0 %copy-start.35 = (f32[768]{0:T(1024)S(1)}, f32[768]{0:T(1024)}, u32[]{:S(2)}) copy-start(f32[768]{0:T(1024)} %param.22) | copy-start | bytes 9220
  135.2 137.5 %copy-start.34 = (f32[768]{0:T(1024)S(1)}, f32[768]{0:T(1024)}, u32[]{:S(2)}) copy-start(f32[768]{0:T(1024)} %param.23) | copy-start | bytes 9220
  135.2 137.5 %copy-start.36 = (f32[768]{0:T(1024)S(1)}, f32[768]{0:T(1024)}, u32[]{:S(2)}) copy-start(f32[768]{0:T(1024)} %param.24) | copy-start | bytes 9220
  135.3 215.9 %all-gather.7.cloned.1.call-start = ((), (), s32[]{:S(2)}) async-start(), calls=%async_computation.6 | async-start | bytes 4915200 | tf_op jit(solution)/shard_map/all_gather | solution.py:182
  274.1 153.6 %all-gather.9.cloned.1.call-start = ((), (), s32[]{:S(2)}) async-start(), calls=%async_computation.8 | async-start | bytes 4915200 | tf_op jit(solution)/shard_map/all_gather | solution.py:195
  274.6 319.0 %reduce-scatter.9.cloned.1.call-start = ((), (), s32[]{:S(2)}) async-start(), calls=%async_computation.9 | async-start | bytes 9830400 | tf_op jit(solution)/shard_map/reduce_scatter | solution.py:199
  427.6 25.7 %copy-start.43 = (bf16[768,768]{1,0:T(8,128)(2,1)S(1)}, bf16[768,768]{1,0:T(8,128)(2,1)}, u32[]{:S(2)}) copy-start(bf16[768,768]{1,0:T(8,128)(2,1)} %param.25) | copy-start | bytes 3538948
  458.7 210.3 %reduce-scatter.7.cloned.1.call-start = ((), (), s32[]{:S(2)}) async-start(), calls=%async_computation.7 | async-start | bytes 4915200 | tf_op jit(solution)/shard_map/reduce_scatter | solution.py:187
  473.8 195.2 %copy-start.37 = (f32[768]{0:T(1024)S(1)}, f32[768]{0:T(1024)}, u32[]{:S(2)}) copy-start(f32[768]{0:T(1024)} %param.28) | copy-start | bytes 9220
  473.9 278.3 %all-gather.11.cloned.1.call-start = ((), (), s32[]{:S(2)}) async-start(), calls=%async_computation.10 | async-start | bytes 4915200 | tf_op jit(solution)/shard_map/all_gather | solution.py:209
  669.0 5.0 copy-start.12
  675.3 201.8 %reduce-scatter.11.cloned.1.call-start = ((), (), s32[]{:S(2)}) async-start(), calls=%async_computation.11 | async-start | bytes 4915200 | tf_op jit(solution)/shard_map/reduce_scatter | solution.py:223
  759.9 7.2 copy-start.2
  805.7 190.8 %all-reduce.5.cloned.1.call-start = ((), (), s32[]{:S(2)}) async-start(), calls=%async_computation.12 | async-start | bytes 14155776 | tf_op jit(solution)/shard_map/psum | solution.py:249
  806.0 8.2 copy-start.16
  806.0 8.2 copy-start.42
  814.2 6.6 copy-start.41
  824.6 52.5 %copy-start.3 = (bf16[640,768]{1,0:T(8,128)(2,1)S(1)}, bf16[640,768]{1,0:T(8,128)(2,1)}, u32[]{:S(2)}) copy-start(bf16[640,768]{1,0:T(8,128)(2,1)} %param.15) | copy-start | bytes 2949124
  824.6 52.5 %copy-start.28 = (f32[640]{0:T(1024)S(1)}, f32[640]{0:T(1024)}, u32[]{:S(2)}) copy-start(f32[640]{0:T(1024)} %copy-done.27) | copy-start | bytes 7684
  824.6 52.5 %copy-start.29 = (f32[768]{0:T(1024)S(1)}, f32[768]{0:T(1024)}, u32[]{:S(2)}) copy-start(f32[768]{0:T(1024)} %param.17) | copy-start | bytes 9220
  826.9 52.3 %copy-start.33 = (f32[640]{0:T(1024)S(1)}, f32[640]{0:T(1024)}, u32[]{:S(2)}) copy-start(f32[640]{0:T(1024)} %copy-done.32) | copy-start | bytes 7684
  826.9 52.3 %copy-start.31 = (f32[640]{0:T(1024)S(1)}, f32[640]{0:T(1024)}, u32[]{:S(2)}) copy-start(f32[640]{0:T(1024)} %copy-done.30) | copy-start | bytes 7684
  827.0 54.6 %copy-start.13 = (bf16[640,768]{1,0:T(8,128)(2,1)S(1)}, bf16[640,768]{1,0:T(8,128)(2,1)}, u32[]{:S(2)}) copy-start(bf16[640,768]{1,0:T(8,128)(2,1)} %param.29) | copy-start | bytes 2949124
  (24 other events, 68.1 us)
Sparse Core Ops, SparseCore 0:
  14.4 79.1 all-gather.4
  135.4 134.8 reduce-scatter.4
  274.2 76.9 all-gather.6
  352.6 74.9 all-gather.8
  458.8 134.8 reduce-scatter.8
  595.8 73.1 reduce-scatter.6
  675.4 76.7 all-gather.10
  805.8 71.2 reduce-scatter.10
  881.9 114.5 all-reduce.4
where the time goes:
time: 1010 us
  waiting for transfers between devices  732 us (72%)
  matrix products  105 us (10%)
  local copies, waits for them, and re-layouts  62.3 us (6%)
  blocking collectives  56.1 us (6%)
  other arithmetic  38.2 us (4%)
  between operations  14.8 us (1%)
    reduce_scatter x1, waiting for transfers between devices, local(): lax.psum_scatter(jnp.dot(blend_low, mixer_weight, preferred_element_type=...  135 us
    reduce_scatter x1, waiting for transfers between devices, local(): lax.psum_scatter(jnp.einsum('rf,df->rd', grad_pre_low, up_weight, preferr...  120 us
    all_gather x1, waiting for transfers between devices, local(): whole_one = lax.all_gather(low_one, 'tensor', axis=0, tiled=True)  79 us
    all_gather x1, waiting for transfers between devices, local(): lax.all_gather(grad_first.astype(jnp.bfloat16), 'tensor', axis=0, tiled=T...  76.9 us
    all_gather x1, waiting for transfers between devices, local(): whole_two = lax.all_gather(low_two, 'tensor', axis=0, tiled=True)  76.5 us
    reduce_scatter x1, waiting for transfers between devices, local(): lax.psum_scatter(jnp.dot(active, down_weight, preferred_element_type=jnp....  73.1 us
    psum x1, waiting for transfers between devices, local(): lax.psum((weight_terms[0], weight_terms[1], weight_terms[2], weight_terms...  71.1 us
    all_gather x1, waiting for transfers between devices, local(): whole_grad = lax.all_gather(output_grad, 'tensor', axis=0, tiled=True)  67.5 us
  transfers between devices with their start and end apart: 9, of which 9 were waited for; matrix products, arithmetic and copies ran while one was open for 5% of the time, Pallas kernels for 0%

commit v1 on v0

--- a/solution.py
+++ b/solution.py
@@ -235,15 +235,18 @@
     grad_tokens = grad_first + grad_inputs
     sum_gain_one, sum_shift_one, sum_mix_bias, sum_gain_two, sum_shift_two, sum_down_bias = (
         lax.psum(
-            (
-                grad_gain_one,
-                grad_shift_one,
-                jnp.sum(grad_first, axis=0),
-                grad_gain_two,
-                grad_shift_two,
-                jnp.sum(grad_output, axis=0),
+            lax.psum(
+                (
+                    grad_gain_one,
+                    grad_shift_one,
+                    jnp.sum(grad_first, axis=0),
+                    grad_gain_two,
+                    grad_shift_two,
+                    jnp.sum(grad_output, axis=0),
+                ),
+                "tensor",
             ),
-            ("dp", "tensor"),
+            "dp",
         )
     )
     sum_weight_in, sum_bias_in, sum_mix, sum_up, sum_up_b, sum_down = lax.psum(

time: 1010 us -> 1010 us (level)
  waiting for transfers between devices: 732 us -> 746 us
  blocking collectives: 56.1 us -> 42.3 us
    psum x1, blocking collectives: 41.7 us -> 18 us  [local(): lax.psum((grad_gain_one, grad_shift_one, jnp.sum(grad_first, axis=0), gra...]
    reduce_scatter x1, waiting for transfers between devices: 33.2 us -> 47.6 us  [local(): lax.psum_scatter(jnp.einsum('rjc,djc->rd', grad_projected, input_weight,...]
where the time goes in v1:
time: 1010 us
  waiting for transfers between devices  746 us (74%)
  matrix products  105 us (10%)
  local copies, waits for them, and re-layouts  62.3 us (6%)
  blocking collectives  42.3 us (4%)
  other arithmetic  38.2 us (4%)
  between operations  14.8 us (1%)
    reduce_scatter x1, waiting for transfers between devices, local(): lax.psum_scatter(jnp.dot(blend_low, mixer_weight, preferred_element_type=...  135 us
    reduce_scatter x1, waiting for transfers between devices, local(): lax.psum_scatter(jnp.einsum('rf,df->rd', grad_pre_low, up_weight, preferr...  120 us
    all_gather x1, waiting for transfers between devices, local(): whole_one = lax.all_gather(low_one, 'tensor', axis=0, tiled=True)  79 us
    all_gather x1, waiting for transfers between devices, local(): lax.all_gather(grad_first.astype(jnp.bfloat16), 'tensor', axis=0, tiled=T...  76.8 us
    all_gather x1, waiting for transfers between devices, local(): whole_two = lax.all_gather(low_two, 'tensor', axis=0, tiled=True)  76.5 us
    reduce_scatter x1, waiting for transfers between devices, local(): lax.psum_scatter(jnp.dot(active, down_weight, preferred_element_type=jnp....  73.1 us
    psum x1, waiting for transfers between devices, local(): lax.psum((weight_terms[0], weight_terms[1], weight_terms[2], weight_terms...  70.1 us
    all_gather x1, waiting for transfers between devices, local(): whole_grad = lax.all_gather(output_grad, 'tensor', axis=0, tiled=True)  67.5 us
  transfers between devices with their start and end apart: 9, of which 9 were waited for; matrix products, arithmetic and copies ran while one was open for 5% of the time, Pallas kernels for 0%

profile of v1, /device:TPU:0, one launch (start us, length us, event | category | flops | bytes accessed | tf_op | source)
XLA Modules:
  0.0 1009.7 jit_solution(15641046415969071522)
XLA Ops:
  14.6 79.0 %all-gather.5.cloned.1.call-done = bf16[2560,768]{1,0:T(8,128)(2,1)} async-done(((bf16[640,768]{1,0:T(8,128)(2,1)}), bf16[2560,768]{1,0:T(8,128)(2,1)}) %all-gather.5.cloned.1.call-update) | async-done | bytes 3932176 | tf_op jit(solution)/shard_map/all_gather | solution.py:165
  93.6 4.6 fusion.6
  104.7 4.7 squeeze.4
  109.4 4.1 squeeze.10
  113.5 5.2 fusion.57
  130.9 4.3 fusion.58
  135.3 134.9 %reduce-scatter.5.cloned.1.call-done = f32[640,768]{1,0:T(8,128)} async-done(((f32[2560,768]{1,0:T(8,128)}), f32[640,768]{1,0:T(8,128)}) %reduce-scatter.5.cloned.1.call-update) | async-done | bytes 1966096 | tf_op jit(solution)/shard_map/reduce_scatter | solution.py:173
  274.7 76.5 %all-gather.7.cloned.1.call-done = bf16[2560,768]{1,0:T(8,128)(2,1)} async-done(((bf16[640,768]{1,0:T(8,128)(2,1)}), bf16[2560,768]{1,0:T(8,128)(2,1)}) %all-gather.7.cloned.1.call-update) | async-done | bytes 3932176 | tf_op jit(solution)/shard_map/all_gather | solution.py:182
  351.2 9.0 fusion.59
  360.2 67.5 %all-gather.9.cloned.1.call-done = bf16[2560,768]{1,0:T(8,128)(2,1)} async-done(((bf16[640,768]{1,0:T(8,128)(2,1)}), bf16[2560,768]{1,0:T(8,128)(2,1)}) %all-gather.9.cloned.1.call-update) | async-done | bytes 3932176 | tf_op jit(solution)/shard_map/all_gather | solution.py:195
  427.6 23.8 %fusion.51 = (f32[768]{0:T(1024)S(1)}, bf16[2560,768]{1,0:T(8,128)(2,1)S(1)}, f32[2560,768]{1,0:T(8,128)}) fusion(f32[2560,768]{1,0:T(8,128)} %fusion.59, f32[768]{0:T(1024)S(1)} %convert_element_type.88, bf16[2560,768]{1,0:T(8,128)(2,1)} %all-gather.9.cloned.1.call-done, bf16[768,768]{1,0:T(8,128)(2,1)S(1)} %copy-done), kind=kOutput, calls=%fused_computation.106 | convolution fusion | flops 3165388032 | bytes 24778752 | tf_op jit(solution)/shard_map/rd,fd->rf/dot_general | solution.py:100
  453.3 5.4 fusion.29
  459.2 8.0 multiply_convert_fusion
  469.1 4.7 convolution_convert_fusion
  473.9 119.8 %reduce-scatter.9.cloned.1.call-done = f32[640,768]{1,0:T(8,128)} async-done(((f32[2560,768]{1,0:T(8,128)}), f32[640,768]{1,0:T(8,128)}) %reduce-scatter.9.cloned.1.call-update) | async-done | bytes 1966096 | tf_op jit(solution)/shard_map/reduce_scatter | solution.py:199
  596.0 73.1 %reduce-scatter.7.cloned.1.call-done = bf16[640,768]{1,0:T(8,128)(2,1)} async-done(((bf16[2560,768]{1,0:T(8,128)(2,1)}), bf16[640,768]{1,0:T(8,128)(2,1)}) %reduce-scatter.7.cloned.1.call-update) | async-done | bytes 983056 | tf_op jit(solution)/shard_map/reduce_scatter | solution.py:187
  669.1 3.7 fusion.53
  675.4 76.8 %all-gather.11.cloned.1.call-done = bf16[2560,768]{1,0:T(8,128)(2,1)} async-done(((bf16[640,768]{1,0:T(8,128)(2,1)}), bf16[2560,768]{1,0:T(8,128)(2,1)}) %all-gather.11.cloned.1.call-update) | async-done | bytes 3932176 | tf_op jit(solution)/shard_map/all_gather | solution.py:209
  752.2 4.5 convolution_convert_fusion.1
  760.0 7.1 multiply_reduce_fusion
  772.0 4.0 fusion.33
  780.6 3.9 stack_reshape.14
  786.9 3.7 stack_reshape.13
  793.0 3.7 stack_reshape.12
  800.9 4.7 bitcast_convert_fusion
  806.0 8.1 fusion.27
  814.2 4.8 fusion.61
  820.9 3.7 fusion.62
  829.5 47.6 %reduce-scatter.11.cloned.1.call-done = bf16[640,768]{1,0:T(8,128)(2,1)} async-done(((bf16[2560,768]{1,0:T(8,128)(2,1)}), bf16[640,768]{1,0:T(8,128)(2,1)}) %reduce-scatter.11.cloned.1.call-update) | async-done | bytes 983056 | tf_op jit(solution)/shard_map/reduce_scatter | solution.py:223
  883.8 18.0 %all-reduce.2 = (f32[768]{0:T(1024)S(1)}, f32[768]{0:T(1024)S(1)}, f32[768]{0:T(1024)S(1)}, f32[768]{0:T(1024)S(1)}, f32[768]{0:T(1024)S(1)}, /*index=5*/f32[768]{0:T(1024)S(1)}) all-reduce(f32[768]{0:T(1024)S(1)} %get-tuple-element.16, f32[768]{0:T(1024)S(1)} %get-tuple-element.21, ...), channel_id=1, replica_groups=mesh['dp'=8,'tensor'=4] {'tensor'}, use_global_device_ids=true, to_apply=%region_16.17 | all-reduce | flops 4608 | bytes 36864 | tf_op jit(solution)/shard_map/psum | solution.py:238
  901.8 24.3 %all-reduce = (f32[768]{0:T(1024)}, f32[768]{0:T(1024)}, f32[2,192]{1,0:T(2,128)}, f32[768]{0:T(1024)}, f32[768]{0:T(1024)}, /*index=5*/f32[768]{0:T(1024)}, f32[768]{0:T(1024)}, f32[768]{0:T(1024)}) all-reduce(f32[768]{0:T(1024)S(1)} %get-tuple-element.37, ...), channel_id=1, replica_groups=mesh['dp'=8,'tensor'=4] {'dp'}, use_global_device_ids=true, to_apply=%region_17.18 | all-reduce | flops 5760 | bytes 46080 | tf_op jit(solution)/shard_map/psum | solution.py:237
  926.1 70.1 %all-reduce.5.cloned.1.call-done = (f32[768,3,192]{0,2,1:T(8,128)}, f32[192,768]{1,0:T(8,128)}, f32[768,768]{1,0:T(8,128)}, f32[768,768]{1,0:T(8,128)}) async-done(((f32[768,3,192]{0,2,1:T(8,128)}, f32[192,768]{1,0:T(8,128)}, f32[768,768]{1,0:T(8,128)}, f32[768,768]{1,0:T(8,128)}), (f32[768,3,192]{0,2,1:T(8,128)}, f32[192,768]{1,0:T(8,128)}, f32[768,768]{1,0:T(8,128)}, ...) | async-done | bytes 7077904 | tf_op jit(solution)/shard_map/psum | solution.py:252
  (164 shorter events, 81.8 us)
Async XLA Ops:
  7.2 420.5 %copy-start = (bf16[768,768]{1,0:T(8,128)(2,1)S(1)}, bf16[768,768]{1,0:T(8,128)(2,1)}, u32[]{:S(2)}) copy-start(bf16[768,768]{1,0:T(8,128)(2,1)} %param.27) | copy-start | bytes 3538948
  7.2 7.1 copy-start.38
  7.2 7.3 copy-start.40
  7.2 86.3 %copy-start.44 = (bf16[768,3,192]{0,2,1:T(8,128)(2,1)S(1)}, bf16[768,3,192]{0,2,1:T(8,128)(2,1)}, u32[]{:S(2)}) copy-start(bf16[768,3,192]{0,2,1:T(8,128)(2,1)} %param.19) | copy-start | bytes 2654212
  7.2 86.3 %all-gather.5.cloned.1.call-start = ((), (), s32[]{:S(2)}) async-start(), calls=%async_computation.4 | async-start | bytes 4915200 | tf_op jit(solution)/shard_map/all_gather | solution.py:165
  14.3 255.9 %reduce-scatter.5.cloned.1.call-start = ((), (), s32[]{:S(2)}) async-start(), calls=%async_computation.5 | async-start | bytes 9830400 | tf_op jit(solution)/shard_map/reduce_scatter | solution.py:173
  104.7 8.9 copy-start.7
  118.8 6.3 copy-start.1
  125.1 5.8 copy-start.24
  135.2 135.0 %copy-start.35 = (f32[768]{0:T(1024)S(1)}, f32[768]{0:T(1024)}, u32[]{:S(2)}) copy-start(f32[768]{0:T(1024)} %param.22) | copy-start | bytes 9220
  135.2 137.5 %copy-start.34 = (f32[768]{0:T(1024)S(1)}, f32[768]{0:T(1024)}, u32[]{:S(2)}) copy-start(f32[768]{0:T(1024)} %param.23) | copy-start | bytes 9220
  135.2 137.5 %copy-start.36 = (f32[768]{0:T(1024)S(1)}, f32[768]{0:T(1024)}, u32[]{:S(2)}) copy-start(f32[768]{0:T(1024)} %param.24) | copy-start | bytes 9220
  135.3 215.9 %all-gather.7.cloned.1.call-start = ((), (), s32[]{:S(2)}) async-start(), calls=%async_computation.6 | async-start | bytes 4915200 | tf_op jit(solution)/shard_map/all_gather | solution.py:182
  274.1 153.6 %all-gather.9.cloned.1.call-start = ((), (), s32[]{:S(2)}) async-start(), calls=%async_computation.8 | async-start | bytes 4915200 | tf_op jit(solution)/shard_map/all_gather | solution.py:195
  274.6 319.0 %reduce-scatter.9.cloned.1.call-start = ((), (), s32[]{:S(2)}) async-start(), calls=%async_computation.9 | async-start | bytes 9830400 | tf_op jit(solution)/shard_map/reduce_scatter | solution.py:199
  427.6 25.7 %copy-start.43 = (bf16[768,768]{1,0:T(8,128)(2,1)S(1)}, bf16[768,768]{1,0:T(8,128)(2,1)}, u32[]{:S(2)}) copy-start(bf16[768,768]{1,0:T(8,128)(2,1)} %param.25) | copy-start | bytes 3538948
  458.7 210.4 %reduce-scatter.7.cloned.1.call-start = ((), (), s32[]{:S(2)}) async-start(), calls=%async_computation.7 | async-start | bytes 4915200 | tf_op jit(solution)/shard_map/reduce_scatter | solution.py:187
  473.8 195.2 %copy-start.37 = (f32[768]{0:T(1024)S(1)}, f32[768]{0:T(1024)}, u32[]{:S(2)}) copy-start(f32[768]{0:T(1024)} %param.28) | copy-start | bytes 9220
  473.9 278.3 %all-gather.11.cloned.1.call-start = ((), (), s32[]{:S(2)}) async-start(), calls=%async_computation.10 | async-start | bytes 4915200 | tf_op jit(solution)/shard_map/all_gather | solution.py:209
  669.0 5.0 copy-start.12
  675.3 201.8 %reduce-scatter.11.cloned.1.call-start = ((), (), s32[]{:S(2)}) async-start(), calls=%async_computation.11 | async-start | bytes 4915200 | tf_op jit(solution)/shard_map/reduce_scatter | solution.py:223
  759.9 7.2 copy-start.2
  805.7 190.4 %all-reduce.5.cloned.1.call-start = ((), (), s32[]{:S(2)}) async-start(), calls=%async_computation.12 | async-start | bytes 14155776 | tf_op jit(solution)/shard_map/psum | solution.py:252
  806.0 8.2 copy-start.16
  806.0 8.2 copy-start.42
  814.2 6.6 copy-start.41
  824.6 52.5 %copy-start.3 = (bf16[640,768]{1,0:T(8,128)(2,1)S(1)}, bf16[640,768]{1,0:T(8,128)(2,1)}, u32[]{:S(2)}) copy-start(bf16[640,768]{1,0:T(8,128)(2,1)} %param.15) | copy-start | bytes 2949124
  824.6 52.5 %copy-start.28 = (f32[640]{0:T(1024)S(1)}, f32[640]{0:T(1024)}, u32[]{:S(2)}) copy-start(f32[640]{0:T(1024)} %copy-done.27) | copy-start | bytes 7684
  824.6 52.5 %copy-start.29 = (f32[768]{0:T(1024)S(1)}, f32[768]{0:T(1024)}, u32[]{:S(2)}) copy-start(f32[768]{0:T(1024)} %param.17) | copy-start | bytes 9220
  826.9 52.3 %copy-start.33 = (f32[640]{0:T(1024)S(1)}, f32[640]{0:T(1024)}, u32[]{:S(2)}) copy-start(f32[640]{0:T(1024)} %copy-done.32) | copy-start | bytes 7684
  826.9 52.3 %copy-start.31 = (f32[640]{0:T(1024)S(1)}, f32[640]{0:T(1024)}, u32[]{:S(2)}) copy-start(f32[640]{0:T(1024)} %copy-done.30) | copy-start | bytes 7684
  827.0 54.6 %copy-start.13 = (bf16[640,768]{1,0:T(8,128)(2,1)S(1)}, bf16[640,768]{1,0:T(8,128)(2,1)}, u32[]{:S(2)}) copy-start(bf16[640,768]{1,0:T(8,128)(2,1)} %param.29) | copy-start | bytes 2949124
  (24 other events, 68.1 us)
Sparse Core Ops, SparseCore 0:
  14.4 79.1 all-gather.4
  135.4 134.8 reduce-scatter.4
  274.2 76.9 all-gather.6
  352.6 74.9 all-gather.8
  458.8 134.8 reduce-scatter.8
  595.8 73.1 reduce-scatter.6
  675.4 76.7 all-gather.10
  805.8 71.2 reduce-scatter.10
  881.9 114.1 all-reduce.4
